TPU v7x, 32 devices: a whole 2x2x4 slice. The times are simulated.
32 devices in a mesh: row: 4 (over z), col: 8 (over y, x, core).
Axes of the slice: x: 2, y: 2, z: 4, core: 2. Of those that a mesh axis runs over, the one named last changes fastest.
Arguments:
- spectra: bfloat16 [1024, 32, 128], P(('row', 'col')), may hold values from -6 to 6
- pair_bins: int32 [1024, 1024], P('row', 'col'), may hold values from 0 to 255
- row_subs: int32 [4, 16], P('row'), may hold values from 0 to 31, as said below
- station_subs: int32 [1024, 8], replicated, may hold values from 0 to 31, as said below
- kernel: bfloat16 [32, 256, 256], replicated, may hold values from -0.375 to 0.375
Outputs:
- spectrum: float32 [32, 32, 256], P(('row', 'col'))
Inputs may be any that keep to these rules, and one draw needn't show every extreme that they name: `row_subs`: each row lists 16 distinct subarrays; each subarray is listed for exactly two row blocks. `station_subs`: each station names 8 distinct subarrays, all listed in row_subs for the station's row block.
All inputs are finite; a program needn't handle non-finite values.
Results may differ from a plain program's by a relative error of at most 0.0039.
Values may be sent and summed in bfloat16 or wider, within the bound.
A program may use at most 64 MiB of HBM per device.

v0:
```python
import math
import jax
import jax.numpy as jnp
from jax import lax
from jax.sharding import PartitionSpec as P

F = 32
NBIN = 256
SUB_DEV = 1


def spread_rows(slot_terms, slot_subs, row_count):
    targets = jnp.arange(row_count, dtype=jnp.int32)
    selector = (targets[:, None] == slot_subs[None, :]).astype(jnp.float32)
    return jnp.dot(selector, slot_terms, precision=lax.Precision.HIGHEST)


def project(owned_bins, kernel):
    velocity_power = jnp.einsum(
        "sfb,fbv->sfv", owned_bins, kernel, preferred_element_type=jnp.float32
    )
    scale = lax.rsqrt(jnp.mean(velocity_power * velocity_power, axis=2, keepdims=True) + 1e-06)
    return velocity_power * scale


def on_device(spectra, pair_bins, row_subs, station_subs, kernel):
    shard_rows = spectra.shape[0]
    col_total = lax.axis_size("col")
    row_index = lax.axis_index("row")
    col_index = lax.axis_index("col")
    row_spectra = lax.all_gather(spectra, "col", axis=0, tiled=True)
    col_spectra = lax.all_gather(spectra, "row", axis=0, tiled=True)
    row_span = row_spectra.shape[0]
    col_span = col_spectra.shape[0]
    slot_subs = row_subs[0]
    slot_count = slot_subs.shape[0]
    row_members = lax.dynamic_slice_in_dim(station_subs, row_index * row_span, row_span, 0)
    positions = jnp.arange(col_span, dtype=jnp.int32)
    col_ids = (
        positions // shard_rows * col_total + col_index
    ) * shard_rows + positions % shard_rows
    col_members = jnp.take(station_subs, col_ids, axis=0)
    row_mask = jnp.any(row_members[None, :, :] == slot_subs[:, None, None], axis=2).astype(
        jnp.bfloat16
    )
    col_mask = jnp.any(col_members[None, :, :] == slot_subs[:, None, None], axis=2).astype(
        jnp.bfloat16
    )
    cross_spec = jnp.einsum(
        "aft,jft->faj", row_spectra, col_spectra, preferred_element_type=jnp.float32
    ).astype(jnp.bfloat16)
    step_rows = math.gcd(row_span, max(1, 2048 // col_span))
    step_count = row_span // step_rows
    bin_ids = jnp.arange(NBIN, dtype=jnp.int32)

    def accumulate(step_index, running):
        first_row = step_index * step_rows
        cross_part = lax.dynamic_slice_in_dim(cross_spec, first_row, step_rows, 1)
        mask_part = lax.dynamic_slice_in_dim(row_mask, first_row, step_rows, 1)
        bins_part = lax.dynamic_slice_in_dim(pair_bins, first_row, step_rows, 0)
        weighted = mask_part[:, None, :, None] * col_mask[:, None, None, :] * cross_part[None]
        onehot = (bins_part.reshape(-1, 1) == bin_ids[None, :]).astype(jnp.bfloat16)
        return running + jnp.dot(
            weighted.reshape(slot_count * F, step_rows * col_span),
            onehot,
            preferred_element_type=jnp.float32,
        )

    partial_value = lax.fori_loop(
        0, step_count, accumulate, jnp.zeros((slot_count * F, NBIN), jnp.float32)
    )
    partial_value = partial_value.reshape(slot_count, F, NBIN)
    freq_part = lax.psum_scatter(partial_value, "col", scatter_dimension=1, tiled=True)
    freq_share = freq_part.shape[1]
    group_rows = SUB_DEV * col_total
    summed = lax.psum_scatter(
        spread_rows(
            freq_part.reshape(slot_count, freq_share * NBIN),
            slot_subs,
            lax.axis_size("row") * group_rows,
        ),
        "row",
        scatter_dimension=0,
        tiled=True,
    )
    binned = summed.reshape(group_rows, freq_share, NBIN).astype(jnp.bfloat16)
    return project(lax.all_to_all(binned, "col", split_axis=0, concat_axis=1, tiled=True), kernel)


def solution(mesh):
    in_specs = (P(("row", "col"), None, None), P("row", "col"), P("row", None), P(), P())
    out_specs = P(("row", "col"), None, None)
    return jax.shard_map(
        on_device, mesh=mesh, in_specs=in_specs, out_specs=out_specs, check_vma=False
    )
```

profile of v0, /device:TPU:0, one launch (start us, length us, event | category | flops | bytes accessed | tf_op | source)
XLA Modules:
  0.0 180.9 jit_solution(14719300169441912463)
XLA Ops:
  6.5 1.8 copy.29
  12.6 27.1 %all-gather.5.cloned.1.call-done = bf16[128,32,128]{2,0,1:T(8,128)(2,1)} async-done(((bf16[32,32,128]{2,0,1:T(8,128)(2,1)}), bf16[128,32,128]{2,0,1:T(8,128)(2,1)}) %all-gather.5.cloned.1.call-update) | async-done | bytes 1048592 | tf_op jit(solution)/shard_map/all_gather | solution.py:32
  39.6 29.4 %all-gather.3.cloned.1.call-done = bf16[256,32,128]{2,0,1:T(8,128)(2,1)} async-done(((bf16[32,32,128]{2,0,1:T(8,128)(2,1)}), bf16[256,32,128]{2,0,1:T(8,128)(2,1)}) %all-gather.3.cloned.1.call-update) | async-done | bytes 2097168 | tf_op jit(solution)/shard_map/all_gather | solution.py:31
  69.0 2.6 %convolution_convert_fusion = bf16[32,256,128]{2,1,0:T(8,128)(2,1)S(1)} fusion(bf16[256,32,128]{2,0,1:T(8,128)(2,1)} %all-gather.3.cloned.1.call-done, bf16[128,32,128]{2,0,1:T(8,128)(2,1)} %all-gather.5.cloned.1.call-done), kind=kOutput, calls=%fused_computation.13 | convolution fusion | flops 269484032 | bytes 5242880 | tf_op jit(solution)/shard_map/aft,jft->faj/dot_general | solution.py:49
  71.6 33.1 %while.14 = (s32[]{:T(128)}, f32[512,256]{1,0:T(8,128)S(1)}, bf16[16,256]{1,0:T(8,128)(2,1)S(1)}, bf16[16,128]{1,0:T(8,128)(2,1)S(1)}, bf16[32,256,128]{2,1,0:T(...) while((s32[]{:T(128)}, f32[512,256]{1,0:T(8,128)S(1)}, ...), condition=%wide.region_3.4_spmd.clone, body=%wide.region_2.3_spmd.clone.sunk | while | flops 538738688 | bytes 5797553 | solution.py:69
  72.7 1.0 fusion.31
  74.8 1.0 fusion.31
  76.8 1.0 fusion.31
  78.9 1.0 fusion.31
  81.0 1.0 fusion.31
  83.0 1.0 fusion.31
  85.1 1.0 fusion.31
  87.2 1.0 fusion.31
  89.3 1.0 fusion.31
  93.4 1.0 fusion.31
  95.5 1.0 fusion.31
  99.6 1.0 fusion.31
  101.7 1.0 fusion.31
  103.8 1.0 fusion.31
  104.8 1.1 copy.31
  105.9 34.2 %reduce-scatter.3.cloned.1.call-done = f32[16,4,256]{2,0,1:T(8,128)} async-done(((f32[16,32,256]{2,0,1:T(8,128)}), f32[16,4,256]{2,0,1:T(8,128)}) %reduce-scatter.3.cloned.1.call-update) | async-done | bytes 65552 | tf_op jit(solution)/shard_map/reduce_scatter | solution.py:73
  141.9 19.9 %reduce-scatter.5.cloned.1.call-done = f32[8,1024]{1,0:T(8,128)} async-done(((f32[32,1024]{1,0:T(8,128)}), f32[8,1024]{1,0:T(8,128)}) %reduce-scatter.5.cloned.1.call-update) | async-done | bytes 32784 | tf_op jit(solution)/shard_map/reduce_scatter | solution.py:76
  162.5 8.2 %all_to_all.4 = bf16[8,4,256]{2,1,0:T(4,128)(2,1)S(1)} all-to-all(bf16[8,4,256]{2,1,0:T(4,128)(2,1)S(1)} %copy.33), channel_id=1, replica_groups=mesh['row'=4,'col'=8] {'col'}, dimensions={0} | all-to-all | bytes 32768 | tf_op jit(solution)/shard_map/all_to_all | solution.py:87
  170.7 2.8 %fusion.22 = f32[32,1,256]{2,1,0:T(1,128)S(1)} fusion(bf16[32,256,1]{1,2,0:T(2,128)(2,1)S(1)} %reshape.159, bf16[32,256,256]{2,1,0:T(8,128)(2,1)} %param.11), kind=kOutput, calls=%fused_computation.49 | convolution fusion | flops 4194304 | bytes 4243456 | tf_op jit(solution)/shard_map/sfb,fbv->sfv/dot_general | solution.py:19
  (113 shorter events, 26.2 us)
Async XLA Ops:
  6.5 5.9 %copy-start = (s32[1,16]{1,0:T(1,128)S(1)}, s32[1,16]{1,0:T(1,128)}, u32[]{:S(2)}) copy-start(s32[1,16]{1,0:T(1,128)} %param.9) | copy-start | bytes 196
  6.5 33.1 %all-gather.5.cloned.1.call-start = ((), (), s32[]{:S(2)}) async-start(), calls=%async_computation.4 | async-start | bytes 1310720 | tf_op jit(solution)/shard_map/all_gather | solution.py:32
  8.3 60.7 %all-gather.3.cloned.1.call-start = ((), (), s32[]{:S(2)}) async-start(), calls=%async_computation.3 | async-start | bytes 2359296 | tf_op jit(solution)/shard_map/all_gather | solution.py:31
  9.1 131.1 %reduce-scatter.3.cloned.1.call-start = ((), (), s32[]{:S(2)}) async-start(), calls=%async_computation.5 | async-start | bytes 589824 | tf_op jit(solution)/shard_map/reduce_scatter | solution.py:73
  105.9 55.8 %reduce-scatter.5.cloned.1.call-start = ((), (), s32[]{:S(2)}) async-start(), calls=%async_computation.6 | async-start | bytes 163840 | tf_op jit(solution)/shard_map/reduce_scatter | solution.py:76
Sparse Core Ops, SparseCore 0:
  8.9 30.6 all-gather.4
  41.5 27.4 all-gather.2
  106.0 34.1 reduce-scatter.2
  142.3 19.4 reduce-scatter.4
where the time goes:
time: 182 us; the launch traced here: 181 us
  waiting for transfers between devices  111 us (61%)
  matrix products  21.9 us (12%)
  local copies, waits for them, and re-layouts  19 us (10%)
  between operations  13.2 us (7%)
  blocking collectives  8.21 us (5%)
  other arithmetic  6.36 us (3%)
    reduce_scatter x1, waiting for transfers between devices, on_device(): lax.psum_scatter(partial_value, 'col', scatter_dimension=1, tiled=True)  34.2 us
    all_gather x1, waiting for transfers between devices, on_device(): row_spectra = lax.all_gather(spectra, 'col', axis=0, tiled=True)  29.4 us
    all_gather x1, waiting for transfers between devices, on_device(): col_spectra = lax.all_gather(spectra, 'row', axis=0, tiled=True)  27.1 us
    reduce_scatter x1, waiting for transfers between devices, on_device(): lax.psum_scatter(spread_rows(freq_part.reshape(slot_count, freq_share * N...  19.9 us
    dot_general x16, matrix products, accumulate(): jnp.dot(weighted.reshape(slot_count * F, step_rows * col_span), onehot, p...  15.6 us
    eq x16, local copies, waits for them, and re-layouts, accumulate(): onehot = (bins_part.reshape(-1, 1) == bin_ids[None, :]).astype(jnp.bfloat16)  11.2 us
    all_to_all x1, blocking collectives, on_device(): lax.all_to_all(binned, 'col', split_axis=0, concat_axis=1, tiled=True)  8.21 us
    mul x32, other arithmetic, accumulate(): mask_part[:, None, :, None] * col_mask[:, None, None, :] * cross_part[None]  3.76 us
  transfers between devices with their start and end apart: 4, of which 4 were waited for; matrix products, arithmetic and copies ran while one was open for 2% of the time, Pallas kernels for 0%

commit v1 on v0

--- a/solution.py
+++ b/solution.py
@@ -28,7 +28,14 @@
     col_total = lax.axis_size("col")
     row_index = lax.axis_index("row")
     col_index = lax.axis_index("col")
-    row_spectra = lax.all_gather(spectra, "col", axis=0, tiled=True)
+    num = lax.axis_size("col")
+    tray = [spectra]
+    for h in range(num - 1):
+        outcome_arr = lax.ppermute(tray[-1], "col", [(m, (m + 1) % num) for m in range(num)])
+        tray.append(outcome_arr)
+    prior = jnp.concatenate(tray[::-1], 0)
+    block_out = lax.axis_index("col")
+    row_spectra = jnp.roll(prior, shift=(block_out + 1) * spectra.shape[0], axis=0)
     col_spectra = lax.all_gather(spectra, "row", axis=0, tiled=True)
     row_span = row_spectra.shape[0]
     col_span = col_spectra.shape[0]

time: 182 us -> 198 us (1.088)
  local copies, waits for them, and re-layouts: 19 us -> 45.6 us
  waiting for transfers between devices: 111 us -> 98.4 us
    ppermute x0 -> x7, waiting for transfers between devices: none -> 42.9 us  [on_device(): lax.ppermute(tray[-1], 'col', [(m, (m + 1) % num) for m in range(num)])]
    all_gather x1 -> x0, waiting for transfers between devices: 29.4 us -> none  [on_device(): row_spectra = lax.all_gather(spectra, 'col', axis=0, tiled=True)]
    all_gather x1, waiting for transfers between devices: 27.1 us -> 0.01 us  [on_device(): col_spectra = lax.all_gather(spectra, 'row', axis=0, tiled=True)]
    dynamic_slice x16, local copies, waits for them, and re-layouts: 0.43 us -> 14.9 us  [accumulate(): cross_part = lax.dynamic_slice_in_dim(cross_spec, first_row, step_rows, 1)]
    unnamed x4 -> x23, local copies, waits for them, and re-layouts: 2.74 us -> 14 us
  transfers between devices with their start and end apart: 4 -> 10, of which waited for: 4 -> 9; matrix products, arithmetic and copies ran while one was open for 2% -> 9% of each run, Pallas kernels for 0% -> 0%
where the time goes in v1:
time: 198 us; the launch traced here: 197 us
  waiting for transfers between devices  98.4 us (50%)
  local copies, waits for them, and re-layouts  45.6 us (23%)
  matrix products  23.1 us (12%)
  between operations  13.2 us (7%)
  blocking collectives  8.15 us (4%)
  other arithmetic  7.06 us (4%)
    ppermute x7, waiting for transfers between devices, on_device(): lax.ppermute(tray[-1], 'col', [(m, (m + 1) % num) for m in range(num)])  42.9 us
    reduce_scatter x1, waiting for transfers between devices, on_device(): lax.psum_scatter(partial_value, 'col', scatter_dimension=1, tiled=True)  35.3 us
    reduce_scatter x1, waiting for transfers between devices, on_device(): lax.psum_scatter(spread_rows(freq_part.reshape(slot_count, freq_share * N...  20.1 us
    dot_general x16, matrix products, accumulate(): jnp.dot(weighted.reshape(slot_count * F, step_rows * col_span), onehot, p...  15.6 us
    dynamic_slice x16, local copies, waits for them, and re-layouts, accumulate(): cross_part = lax.dynamic_slice_in_dim(cross_spec, first_row, step_rows, 1)  14.9 us
    unnamed x23, local copies, waits for them, and re-layouts  14 us
    eq x16, local copies, waits for them, and re-layouts, accumulate(): onehot = (bins_part.reshape(-1, 1) == bin_ids[None, :]).astype(jnp.bfloat16)  11.3 us
    all_to_all x1, blocking collectives, on_device(): lax.all_to_all(binned, 'col', split_axis=0, concat_axis=1, tiled=True)  8.15 us
  transfers between devices with their start and end apart: 10, of which 9 were waited for; matrix products, arithmetic and copies ran while one was open for 9% of the time, Pallas kernels for 0%

profile of v1, /device:TPU:0, one launch (start us, length us, event | category | flops | bytes accessed | tf_op | source)
XLA Modules:
  0.0 196.9 jit_solution(11725139641559954471)
XLA Ops:
  6.5 1.1 copy.37
  8.2 6.9 %collective-permute-done = bf16[32,32,128]{2,0,1:T(8,128)(2,1)S(1)} collective-permute-done((bf16[32,32,128]{2,0,1:T(8,128)(2,1)S(1)}, bf16[32,32,128]{2,0,1:T(8,128)(2,1)S(1)}, u32[]{:S(2)}, u32[]{:S(2)}) %collective-permute-start) | collective-permute-done | bytes 262176 | tf_op jit(solution)/shard_map/ppermute | solution.py:34
  15.1 6.7 %collective-permute-done.1 = bf16[32,32,128]{2,0,1:T(8,128)(2,1)S(1)} collective-permute-done((bf16[32,32,128]{2,0,1:T(8,128)(2,1)S(1)}, bf16[32,32,128]{2,0,1:T(8,128)(2,1)S(1)}, u32[]{:S(2)}, u32[]{:S(2)}) %collective-permute-start.1) | collective-permute-done | bytes 262176 | tf_op jit(solution)/shard_map/ppermute | solution.py:34
  21.8 6.7 %collective-permute-done.2 = bf16[32,32,128]{2,0,1:T(8,128)(2,1)S(1)} collective-permute-done((bf16[32,32,128]{2,0,1:T(8,128)(2,1)S(1)}, bf16[32,32,128]{2,0,1:T(8,128)(2,1)S(1)}, u32[]{:S(2)}, u32[]{:S(2)}) %collective-permute-start.2) | collective-permute-done | bytes 262176 | tf_op jit(solution)/shard_map/ppermute | solution.py:34
  28.5 6.7 %collective-permute-done.3 = bf16[32,32,128]{2,0,1:T(8,128)(2,1)S(1)} collective-permute-done((bf16[32,32,128]{2,0,1:T(8,128)(2,1)S(1)}, bf16[32,32,128]{2,0,1:T(8,128)(2,1)S(1)}, u32[]{:S(2)}, u32[]{:S(2)}) %collective-permute-start.3) | collective-permute-done | bytes 262176 | tf_op jit(solution)/shard_map/ppermute | solution.py:34
  36.8 5.1 %collective-permute-done.4 = bf16[32,32,128]{2,0,1:T(8,128)(2,1)S(1)} collective-permute-done((bf16[32,32,128]{2,0,1:T(8,128)(2,1)S(1)}, bf16[32,32,128]{2,0,1:T(8,128)(2,1)S(1)}, u32[]{:S(2)}, u32[]{:S(2)}) %collective-permute-start.4) | collective-permute-done | bytes 262176 | tf_op jit(solution)/shard_map/ppermute | solution.py:34
  43.6 5.0 %collective-permute-done.5 = bf16[32,32,128]{2,0,1:T(8,128)(2,1)S(1)} collective-permute-done((bf16[32,32,128]{2,0,1:T(8,128)(2,1)S(1)}, bf16[32,32,128]{2,0,1:T(8,128)(2,1)S(1)}, u32[]{:S(2)}, u32[]{:S(2)}) %collective-permute-start.5) | collective-permute-done | bytes 262176 | tf_op jit(solution)/shard_map/ppermute | solution.py:34
  49.6 5.8 %collective-permute-done.6 = bf16[32,32,128]{2,0,1:T(8,128)(2,1)S(1)} collective-permute-done((bf16[32,32,128]{2,0,1:T(8,128)(2,1)S(1)}, bf16[32,32,128]{2,0,1:T(8,128)(2,1)S(1)}, u32[]{:S(2)}, u32[]{:S(2)}) %collective-permute-start.6) | collective-permute-done | bytes 262176 | tf_op jit(solution)/shard_map/ppermute | solution.py:34
  68.1 3.9 %fusion.11 = bf16[32,256,128]{2,1,0:T(8,128)(2,1)} fusion(bf16[128,32,128]{2,0,1:T(8,128)(2,1)} %all-gather.2.cloned.1.call-done, bf16[512,32,128]{2,0,1:T(8,128)(2,1)} %constant_dynamic-update-slice_fusion, s32[]{:T(128)S(6)} %select_n.90), kind=kOutput, calls=%fused_computation.15 | convolution fusion | flops 269484032 | bytes 5242884 | tf_op jit(solution)/shard_map/aft,jft->faj/dot_general | solution.py:56
  72.0 47.5 %while.14 = (s32[]{:T(128)}, f32[512,256]{1,0:T(8,128)S(1)}, bf16[16,256]{1,0:T(8,128)(2,1)S(1)}, bf16[16,128]{1,0:T(8,128)(2,1)S(1)}, bf16[32,256,128]{2,1,0:T(...) while((s32[]{:T(128)}, f32[512,256]{1,0:T(8,128)S(1)}, ...), condition=%wide.region_3.4_spmd.clone, body=%wide.region_2.3_spmd.clone.sunk | while | flops 538738688 | bytes 5797545 | solution.py:76
  73.9 1.0 fusion.36
  76.9 1.0 fusion.36
  79.9 1.0 fusion.36
  82.8 1.0 fusion.36
  85.8 1.0 fusion.36
  91.8 1.0 fusion.36
  97.7 1.0 fusion.36
  112.6 1.0 fusion.36
  118.5 1.0 fusion.36
  119.5 1.1 copy.41
  120.7 35.3 %reduce-scatter.3.cloned.1.call-done = f32[16,4,256]{2,0,1:T(8,128)} async-done(((f32[16,32,256]{2,0,1:T(8,128)}), f32[16,4,256]{2,0,1:T(8,128)}) %reduce-scatter.3.cloned.1.call-update) | async-done | bytes 65552 | tf_op jit(solution)/shard_map/reduce_scatter | solution.py:80
  157.7 20.1 %reduce-scatter.5.cloned.1.call-done = f32[8,1024]{1,0:T(8,128)} async-done(((f32[32,1024]{1,0:T(8,128)}), f32[8,1024]{1,0:T(8,128)}) %reduce-scatter.5.cloned.1.call-update) | async-done | bytes 32784 | tf_op jit(solution)/shard_map/reduce_scatter | solution.py:83
  178.6 8.2 %all_to_all.4 = bf16[8,4,256]{2,1,0:T(4,128)(2,1)S(1)} all-to-all(bf16[8,4,256]{2,1,0:T(4,128)(2,1)S(1)} %copy.43), channel_id=1, replica_groups=mesh['row'=4,'col'=8] {'col'}, dimensions={0} | all-to-all | bytes 32768 | tf_op jit(solution)/shard_map/all_to_all | solution.py:94
  186.7 2.8 %fusion.28 = f32[32,1,256]{2,1,0:T(1,128)S(1)} fusion(bf16[32,256,1]{1,2,0:T(2,128)(2,1)S(1)} %reshape.159, bf16[32,256,256]{2,1,0:T(8,128)(2,1)} %param.11), kind=kOutput, calls=%fused_computation.68 | convolution fusion | flops 4194304 | bytes 4243456 | tf_op jit(solution)/shard_map/sfb,fbv->sfv/dot_general | solution.py:19
  (144 shorter events, 58.8 us)
Async XLA Ops:
  6.5 54.3 %copy-start = (bf16[32,32,128]{2,1,0:T(8,128)(2,1)S(1)}, bf16[32,32,128]{2,1,0:T(8,128)(2,1)}, u32[]{:S(2)}) copy-start(bf16[32,32,128]{2,1,0:T(8,128)(2,1)} %param.7) | copy-start | bytes 786436
  6.5 61.5 %all-gather.2.cloned.1.call-start = ((), (), s32[]{:S(2)}) async-start(), calls=%async_computation.3 | async-start | bytes 1310720 | tf_op jit(solution)/shard_map/all_gather | solution.py:39
  7.7 27.6 %copy-start.1 = (bf16[32,32,128]{2,0,1:T(8,128)(2,1)}, bf16[32,32,128]{2,0,1:T(8,128)(2,1)S(1)}, u32[]{:S(2)}) copy-start(bf16[32,32,128]{2,0,1:T(8,128)(2,1)S(1)} %copy.37) | copy-start | bytes 786436
  7.7 7.5 %collective-permute-start = (bf16[32,32,128]{2,0,1:T(8,128)(2,1)S(1)}, bf16[32,32,128]{2,0,1:T(8,128)(2,1)S(1)}, u32[]{:S(2)}, u32[]{:S(2)}) collective-permute-start(bf16[32,32,128]{2,0,1:T(8,128)(2,1)S(1)} %copy.37), channel_id=1, source_target_pairs={{0,1},{1,2},{2,3},{3,4},{4,5},{5,6},{6,7},{7,0},{8,9},{9,10},{10,1... | collective-permute-start | bytes 786440 | tf_op jit(solution)/shard_map/ppermute | solution.py:34
  15.1 6.7 %collective-permute-start.1 = (bf16[32,32,128]{2,0,1:T(8,128)(2,1)S(1)}, bf16[32,32,128]{2,0,1:T(8,128)(2,1)S(1)}, u32[]{:S(2)}, u32[]{:S(2)}) collective-permute-start(bf16[32,32,128]{2,0,1:T(8,128)(2,1)S(1)} %collective-permute-done), channel_id=1, source_target_pairs={{0,1},{1,2},{2,3},{3,4},{4,5},{5,6},{6,7},{7,0},{8,9},{9,10},{10,1... | collective-permute-start | bytes 786440 | tf_op jit(solution)/shard_map/ppermute | solution.py:34
  21.8 6.7 %collective-permute-start.2 = (bf16[32,32,128]{2,0,1:T(8,128)(2,1)S(1)}, bf16[32,32,128]{2,0,1:T(8,128)(2,1)S(1)}, u32[]{:S(2)}, u32[]{:S(2)}) collective-permute-start(bf16[32,32,128]{2,0,1:T(8,128)(2,1)S(1)} %collective-permute-done.1), channel_id=1, source_target_pairs={{0,1},{1,2},{2,3},{3,4},{4,5},{5,6},{6,7},{7,0},{8,9},{9,10},{10,1... | collective-permute-start | bytes 786440 | tf_op jit(solution)/shard_map/ppermute | solution.py:34
  28.5 6.7 %collective-permute-start.3 = (bf16[32,32,128]{2,0,1:T(8,128)(2,1)S(1)}, bf16[32,32,128]{2,0,1:T(8,128)(2,1)S(1)}, u32[]{:S(2)}, u32[]{:S(2)}) collective-permute-start(bf16[32,32,128]{2,0,1:T(8,128)(2,1)S(1)} %collective-permute-done.2), channel_id=1, source_target_pairs={{0,1},{1,2},{2,3},{3,4},{4,5},{5,6},{6,7},{7,0},{8,9},{9,10},{10,1... | collective-permute-start | bytes 786440 | tf_op jit(solution)/shard_map/ppermute | solution.py:34
  35.2 6.7 %collective-permute-start.4 = (bf16[32,32,128]{2,0,1:T(8,128)(2,1)S(1)}, bf16[32,32,128]{2,0,1:T(8,128)(2,1)S(1)}, u32[]{:S(2)}, u32[]{:S(2)}) collective-permute-start(bf16[32,32,128]{2,0,1:T(8,128)(2,1)S(1)} %collective-permute-done.3), channel_id=1, source_target_pairs={{0,1},{1,2},{2,3},{3,4},{4,5},{5,6},{6,7},{7,0},{8,9},{9,10},{10,1... | collective-permute-start | bytes 786440 | tf_op jit(solution)/shard_map/ppermute | solution.py:34
  35.3 120.7 %reduce-scatter.3.cloned.1.call-start = ((), (), s32[]{:S(2)}) async-start(), calls=%async_computation.4 | async-start | bytes 589824 | tf_op jit(solution)/shard_map/reduce_scatter | solution.py:80
  41.9 6.7 %collective-permute-start.5 = (bf16[32,32,128]{2,0,1:T(8,128)(2,1)S(1)}, bf16[32,32,128]{2,0,1:T(8,128)(2,1)S(1)}, u32[]{:S(2)}, u32[]{:S(2)}) collective-permute-start(bf16[32,32,128]{2,0,1:T(8,128)(2,1)S(1)} %collective-permute-done.4), channel_id=1, source_target_pairs={{0,1},{1,2},{2,3},{3,4},{4,5},{5,6},{6,7},{7,0},{8,9},{9,10},{10,1... | collective-permute-start | bytes 786440 | tf_op jit(solution)/shard_map/ppermute | solution.py:34
  48.6 6.7 %collective-permute-start.6 = (bf16[32,32,128]{2,0,1:T(8,128)(2,1)S(1)}, bf16[32,32,128]{2,0,1:T(8,128)(2,1)S(1)}, u32[]{:S(2)}, u32[]{:S(2)}) collective-permute-start(bf16[32,32,128]{2,0,1:T(8,128)(2,1)S(1)} %collective-permute-done.5), channel_id=1, source_target_pairs={{0,1},{1,2},{2,3},{3,4},{4,5},{5,6},{6,7},{7,0},{8,9},{9,10},{10,1... | collective-permute-start | bytes 786440 | tf_op jit(solution)/shard_map/ppermute | solution.py:34
  72.0 84.9 %copy-start.2 = (s32[1,16]{1,0:T(1,128)S(1)}, s32[1,16]{1,0:T(1,128)}, u32[]{:S(2)}) copy-start(s32[1,16]{1,0:T(1,128)} %param.9) | copy-start | bytes 196
  120.6 57.2 %reduce-scatter.5.cloned.1.call-start = ((), (), s32[]{:S(2)}) async-start(), calls=%async_computation.5 | async-start | bytes 163840 | tf_op jit(solution)/shard_map/reduce_scatter | solution.py:83
Sparse Core Ops, SparseCore 0:
  35.4 30.2 all-gather.1
  120.7 35.2 reduce-scatter.2
  158.2 19.4 reduce-scatter.4
